TPU v7x, 128 devices: a whole 4x4x4 slice. The times are simulated.
128 devices in a mesh: row: 8 (over y, z_hi), col: 16 (over x, z_lo, core).
Axes of the slice: x: 4, y: 4, z: 4 (z_hi: 2, z_lo: 2; z = z_hi * 2 + z_lo), core: 2. Of those that a mesh axis runs over, the one named last changes fastest.
Arguments:
- factor_blocks: bfloat16 [6, 4, 2048, 2, 4096], P(None, None, 'row', None, 'col'), may hold values from -0.03125 to 0.03125
- inverse_blocks: bfloat16 [4, 2, 4096, 4, 2048], P(None, None, 'col', None, 'row'), as said below
- right_side: bfloat16 [4, 4, 2048, 128], P(None, None, 'row'), may hold values from -4 to 4
- centers: bfloat16 [8, 4096, 512], P(None, 'col')
- owner_map: int32 [8, 16], P(None, 'col'), may hold values from 0 to 7, as said below
- test_pool: bfloat16 [49152, 512], P('row')
- test_rows: int32 [32768], P('row'), may hold values from 0 to 49151, as said below
Outputs:
- coefficients: float32 [4, 2, 4096, 128], P(None, None, 'col')
- predictions: float32 [32768, 128], P(('row', 'col'))
Inputs may be any that keep to these rules, and one draw needn't show every extreme that they name: `owner_map`: each column c is a permutation of 0 to 7. `test_rows`: entry i names a row of block i // 4096 of the pool, that is from (i // 4096) * 6144 to (i // 4096 + 1) * 6144 - 1; rows may repeat. `inverse_blocks`: read as D_k, each block is upper triangular with a positive diagonal.
All inputs are finite; a program needn't handle non-finite values.
Results may differ from a plain program's by a relative error of at most 0.019.
Values may be sent and summed in bfloat16 or wider, within the bound.
A program may use at most 128 MiB of HBM per device.

v0:
```python
import jax
import jax.numpy as jnp
from jax import lax
from jax.sharding import PartitionSpec as P

inverse_width = 0.35


def pair_slot(early, successor):
    return successor * (successor - 1) // 2 + early


def shards(factor_blocks, inverse_blocks, right_side, centers, owner_map, test_pool, test_rows):
    panels = inverse_blocks.shape[0]
    col_tiles = inverse_blocks.shape[1]
    tile_size = inverse_blocks.shape[2]
    row_tiles = inverse_blocks.shape[3]
    width_out = right_side.shape[3]
    own_rows = row_tiles * tile_size
    own_cols = col_tiles * tile_size
    blocks = factor_blocks.reshape(factor_blocks.shape[0], own_rows, own_cols)
    inverse = inverse_blocks.reshape(panels, own_cols, own_rows)
    targets = right_side.reshape(panels, own_rows, width_out)
    solved = [None] * panels
    rounded = [None] * panels

    def subtract(current, partial_value):
        summed = lax.psum(partial_value, "col")
        return (targets[current].astype(jnp.float32) - summed).astype(jnp.bfloat16)

    def settle(current, partial_value):
        if partial_value is None:
            residue = targets[current]
        else:
            residue = subtract(current, partial_value)
        product_rows = jnp.dot(inverse[current], residue, preferred_element_type=jnp.float32)
        summed_rows = lax.psum(product_rows, "row")
        solved[current] = summed_rows
        rounded[current] = summed_rows.astype(jnp.bfloat16)

    final = panels - 1
    for current in range(final, -1, -1):
        partial_value = None
        for successor in range(current + 1, panels):
            product = jnp.dot(
                blocks[pair_slot(current, successor)],
                rounded[successor],
                preferred_element_type=jnp.float32,
            )
            partial_value = product if partial_value is None else partial_value + product
        settle(current, partial_value)
    coefficient = jnp.stack(rounded).reshape(panels * col_tiles, tile_size, width_out)
    paired = jnp.take(coefficient, owner_map[:, 0], axis=0).reshape(panels * own_cols, width_out)
    located = test_rows - lax.axis_index("row") * test_pool.shape[0]
    span_rows = jnp.take(test_pool, located, axis=0)
    flat_centers = centers.reshape(centers.shape[0] * centers.shape[1], centers.shape[2])
    center_sq = jnp.sum(jnp.square(flat_centers.astype(jnp.float32)), axis=1)
    test_sq = jnp.sum(jnp.square(span_rows.astype(jnp.float32)), axis=1)
    crossed = lax.dot_general(
        span_rows, flat_centers, (((1,), (1,)), ((), ())), preferred_element_type=jnp.float32
    )
    distance = test_sq[:, None] + center_sq[None, :] - 2.0 * crossed
    kernel = jnp.exp(-inverse_width * distance).astype(jnp.bfloat16)
    estimate = lax.psum_scatter(
        jnp.dot(kernel, paired, preferred_element_type=jnp.float32).astype(jnp.bfloat16),
        "col",
        scatter_dimension=0,
        tiled=True,
    ).astype(jnp.float32)
    alpha = jnp.stack(solved).reshape(panels, col_tiles, tile_size, width_out)
    return (alpha, estimate)


def solution(mesh):
    in_specs = (
        P(None, None, "row", None, "col"),
        P(None, None, "col", None, "row"),
        P(None, None, "row", None),
        P(None, "col", None),
        P(None, "col"),
        P("row", None),
        P("row"),
    )
    out_specs = (P(None, None, "col", None), P(("row", "col"), None))
    return jax.shard_map(shards, mesh=mesh, in_specs=in_specs, out_specs=out_specs, check_vma=False)
```

profile of v0, /device:TPU:1, one launch (start us, length us, event | category | flops | bytes accessed | tf_op | source)
XLA Modules:
  0.0 815.9 jit_solution(17087823225732025983)
XLA Ops:
  7.2 4.0 fusion.20
  13.6 7.2 fusion.19
  20.8 1.2 copy.20
  22.0 74.3 %all-reduce.8.cloned.1.call-done = f32[512,128]{1,0:T(8,128)} async-done(((f32[512,128]{1,0:T(8,128)}), f32[512,128]{1,0:T(8,128)}) %all-reduce.8.cloned.1.call-update) | async-done | bytes 262160 | tf_op jit(solution)/shard_map/psum | solution.py:37
  96.3 2.5 convolution_bitcast_fusion
  98.9 2.4 copy.19
  101.3 119.3 %all-reduce.10.cloned.1.call-done = f32[1024,128]{1,0:T(8,128)} async-done(((f32[1024,128]{1,0:T(8,128)}), f32[1024,128]{1,0:T(8,128)}) %all-reduce.10.cloned.1.call-update) | async-done | bytes 524304 | tf_op jit(solution)/shard_map/psum | solution.py:28
  220.6 2.5 convolution_bitcast_fusion.3
  223.2 2.6 copy.18
  225.8 2.5 copy.22
  228.7 75.0 %all-reduce.12.cloned.1.call-done = f32[512,128]{1,0:T(8,128)} async-done(((f32[512,128]{1,0:T(8,128)}), f32[512,128]{1,0:T(8,128)}) %all-reduce.12.cloned.1.call-update) | async-done | bytes 262160 | tf_op jit(solution)/shard_map/psum | solution.py:37
  303.7 1.7 fusion.15
  305.4 2.5 fusion
  308.0 2.5 copy.17
  310.6 1.2 copy.16
  312.0 1.2 copy.24
  314.7 21.0 %gather_fusion = bf16[4096,512]{1,0:T(8,128)(2,1)} fusion(bf16[6144,512]{1,0:T(8,128)(2,1)} %param.12, s32[4096]{0:T(1024)S(1)} %fusion.10), kind=kCustom, calls=%fused_computation | custom fusion | bytes 8404992 | tf_op jit(solution)/shard_map/jit(_take)/gather | solution.py:55
  335.8 93.9 %all-reduce.14.cloned.1.call-done = f32[1024,128]{1,0:T(8,128)} async-done(((f32[1024,128]{1,0:T(8,128)}), f32[1024,128]{1,0:T(8,128)}) %all-reduce.14.cloned.1.call-update) | async-done | bytes 524304 | tf_op jit(solution)/shard_map/psum | solution.py:28
  429.7 2.6 convolution_bitcast_fusion.2
  432.3 3.4 multiply_reduce_fusion
  435.7 77.3 %all-reduce.16.cloned.1.call-done = f32[512,128]{1,0:T(8,128)} async-done(((f32[512,128]{1,0:T(8,128)}), f32[512,128]{1,0:T(8,128)}) %all-reduce.16.cloned.1.call-update) | async-done | bytes 262160 | tf_op jit(solution)/shard_map/psum | solution.py:37
  513.0 1.5 fusion.8
  514.5 1.5 convolution_add_fusion.1
  516.0 1.2 fusion.1
  518.1 120.8 %all-reduce.18.cloned.1.call-done = f32[1024,128]{1,0:T(8,128)} async-done(((f32[1024,128]{1,0:T(8,128)}), f32[1024,128]{1,0:T(8,128)}) %all-reduce.18.cloned.1.call-update) | async-done | bytes 524304 | tf_op jit(solution)/shard_map/psum | solution.py:28
  639.0 2.3 convolution_bitcast_fusion.1
  642.7 79.8 %all-reduce.20.cloned.1.call-done = f32[512,128]{1,0:T(8,128)} async-done(((f32[512,128]{1,0:T(8,128)}), f32[512,128]{1,0:T(8,128)}) %all-reduce.20.cloned.1.call-update) | async-done | bytes 262160 | tf_op jit(solution)/shard_map/psum | solution.py:37
  724.5 1.5 gather_fusion.1
  726.0 2.2 bitcast_select_fusion
  728.2 17.1 %convolution_convert_fusion = bf16[4096,128]{1,0:T(8,128)(2,1)} fusion(bf16[2048,128]{1,0:T(8,128)(2,1)} %bitcast_select_fusion, bf16[2048,512]{1,0:T(8,128)(2,1)S(1)} %bitcast.110, f32[2048]{0:T(1024)} %bitcast.118, f32[4096]{0:T(1024)S(1)} %multiply_reduce_fusion, bf16[4096,512]{1,0:T(8,128)(2,1)} %gather_fusion, pred[4096]{0:T(1024)(128)(4,1)} %copy-done.12), kind=kOutput, calls=%fused_computation.4 | convolution fusion | flops 10781982720 | bytes 7892992 | tf_op jit(solution)/shard_map/dot_general | solution.py:65
  746.4 61.2 %reduce-scatter.2.cloned.1.call-done = bf16[256,128]{1,0:T(8,128)(2,1)} async-done(((bf16[4096,128]{1,0:T(8,128)(2,1)}), bf16[256,128]{1,0:T(8,128)(2,1)}) %reduce-scatter.2.cloned.1.call-update) | async-done | bytes 65552 | tf_op jit(solution)/shard_map/reduce_scatter | solution.py:64
  807.5 1.5 convert_element_type.72
  (64 shorter events, 10.2 us)
Async XLA Ops:
  7.2 4.3 copy-start.8
  7.2 89.2 %all-reduce.8.cloned.1.call-start = ((), (), s32[]{:S(2)}) async-start(), calls=%async_computation.1 | async-start | bytes 524288 | tf_op jit(solution)/shard_map/psum | solution.py:37
  13.6 207.0 %all-reduce.10.cloned.1.call-start = ((), (), s32[]{:S(2)}) async-start(), calls=%async_computation.2 | async-start | bytes 1048576 | tf_op jit(solution)/shard_map/psum | solution.py:28
  20.8 199.8 %copy-start.10 = (bf16[1,4,256,128]{3,2,1,0:T(8,128)(2,1)S(1)}, bf16[1,4,256,128]{3,2,1,0:T(8,128)(2,1)}, u32[]{:S(2)}) copy-start(bf16[1,4,256,128]{3,2,1,0:T(8,128)(2,1)} %get-tuple-element.15) | copy-start | bytes 786436
  98.8 204.9 %all-reduce.12.cloned.1.call-start = ((), (), s32[]{:S(2)}) async-start(), calls=%async_computation.3 | async-start | bytes 524288 | tf_op jit(solution)/shard_map/psum | solution.py:37
  223.1 82.3 %copy-start = (f32[512,128]{1,0:T(8,128)S(1)}, f32[512,128]{1,0:T(8,128)}, u32[]{:S(2)}) copy-start(f32[512,128]{1,0:T(8,128)} %all-reduce.8.cloned.1.call-done) | copy-start | bytes 786436
  223.1 206.5 %all-reduce.14.cloned.1.call-start = ((), (), s32[]{:S(2)}) async-start(), calls=%async_computation.4 | async-start | bytes 1048576 | tf_op jit(solution)/shard_map/psum | solution.py:28
  223.2 5.1 copy-start.6
  225.8 82.2 %copy-start.13 = (s32[8,1]{0,1:T(1,128)S(1)}, s32[8,1]{0,1:T(1,128)}, u32[]{:S(2)}) copy-start(s32[8,1]{0,1:T(1,128)} %param.11) | copy-start | bytes 100
  308.0 205.1 %all-reduce.16.cloned.1.call-start = ((), (), s32[]{:S(2)}) async-start(), calls=%async_computation.5 | async-start | bytes 524288 | tf_op jit(solution)/shard_map/psum | solution.py:37
  308.0 5.2 copy-start.4
  310.6 4.2 copy-start.11
  335.7 177.3 %copy-start.1 = (bf16[128,8,2,256]{3,1,2,0:T(8,128)(2,1)S(1)}, bf16[128,8,2,256]{3,1,2,0:T(8,128)(2,1)}, u32[]{:S(2)}) copy-start(bf16[128,8,2,256]{3,1,2,0:T(8,128)(2,1)} %copy.16) | copy-start | bytes 3145732
  335.7 178.8 %copy-start.12 = (pred[4096]{0:T(1024)(128)(4,1)}, pred[4096]{0:T(1024)(128)(4,1)S(1)}, u32[]{:S(2)}) copy-start(pred[4096]{0:T(1024)(128)(4,1)S(1)} %compare_and_fusion) | copy-start | bytes 12292
  432.3 206.7 %all-reduce.18.cloned.1.call-start = ((), (), s32[]{:S(2)}) async-start(), calls=%async_computation.6 | async-start | bytes 1048576 | tf_op jit(solution)/shard_map/psum | solution.py:28
  513.0 3.0 copy-start.2
  514.5 126.8 %copy-start.3 = (f32[512,128]{1,0:T(8,128)S(1)}, f32[512,128]{1,0:T(8,128)}, u32[]{:S(2)}) copy-start(f32[512,128]{1,0:T(8,128)} %all-reduce.12.cloned.1.call-done) | copy-start | bytes 786436
  514.5 127.5 %copy-start.5 = (f32[512,128]{1,0:T(8,128)S(1)}, f32[512,128]{1,0:T(8,128)}, u32[]{:S(2)}) copy-start(f32[512,128]{1,0:T(8,128)} %all-reduce.16.cloned.1.call-done) | copy-start | bytes 786436
  517.3 205.2 %all-reduce.20.cloned.1.call-start = ((), (), s32[]{:S(2)}) async-start(), calls=%async_computation.7 | async-start | bytes 524288 | tf_op jit(solution)/shard_map/psum | solution.py:37
  641.2 87.0 %copy-start.7 = (bf16[8,256,512]{2,1,0:T(8,128)(2,1)S(1)}, bf16[8,256,512]{2,1,0:T(8,128)(2,1)}, u32[]{:S(2)}) copy-start(bf16[8,256,512]{2,1,0:T(8,128)(2,1)} %param.10) | copy-start | bytes 6291460
  641.3 166.3 %reduce-scatter.2.cloned.1.call-start = ((), (), s32[]{:S(2)}) async-start(), calls=%async_computation.8 | async-start | bytes 1114112 | tf_op jit(solution)/shard_map/reduce_scatter | solution.py:64
  728.2 17.1 %copy-start.9 = (f32[512,128]{1,0:T(8,128)S(1)}, f32[512,128]{1,0:T(8,128)}, u32[]{:S(2)}) copy-start(f32[512,128]{1,0:T(8,128)} %all-reduce.20.cloned.1.call-done) | copy-start | bytes 786436
Sparse Core Ops, SparseCore 0:
  13.7 82.6 all-reduce.7
  99.0 121.5 all-reduce.9
  223.2 80.3 all-reduce.11
  308.1 121.5 all-reduce.13
  432.6 80.4 all-reduce.15
  517.4 121.5 all-reduce.17
  642.0 80.4 all-reduce.19
  745.4 62.0 reduce-scatter.1
where the time goes:
time: 819 us; the launch traced here: 816 us
  waiting for transfers between devices  702 us (86%)
  local copies, waits for them, and re-layouts  50.3 us (6%)
  matrix products  36.4 us (4%)
  between operations  14.3 us (2%)
  other arithmetic  12.6 us (2%)
    psum x3, waiting for transfers between devices, subtract(): summed = lax.psum(partial_value, 'col')  334 us
    psum x4, waiting for transfers between devices, settle(): summed_rows = lax.psum(product_rows, 'row')  306 us
    reduce_scatter x1, waiting for transfers between devices, shards(): lax.psum_scatter(jnp.dot(kernel, paired, preferred_element_type=jnp.float...  61.2 us
    gather x1, local copies, waits for them, and re-layouts, shards(): span_rows = jnp.take(test_pool, located, axis=0)  21 us
    dot_general x1, matrix products, shards(): jnp.dot(kernel, paired, preferred_element_type=jnp.float32)  17.1 us
  transfers between devices with their start and end apart: 8, of which 8 were waited for; matrix products, arithmetic and copies ran while one was open for 6% of the time, Pallas kernels for 0%

commit v1 on v0

v1 whole, which is shorter than its diff:
```python
import functools

import jax
import jax.numpy as jnp
from jax import lax
from jax.experimental import pallas as pl
from jax.experimental.pallas import tpu as pltpu
from jax.sharding import PartitionSpec as P

MESH = pl.DeviceIdType.MESH
F32 = jnp.float32
BF16 = jnp.bfloat16
SLOPE = -0.35 * 1.4426950408889634
ROWS_ITEM = 256


def kernel(
    owner, rows, f_hbm, d_hbm, b_hbm, cen_hbm, pool_hbm,
    alpha, pred,
    f_raw, d_raw, f_mat, d_mat, tmp32, y_buf, b_buf, cen, csq, pool_in, pool32,
    stage32, k_mat, x_buf, p32, p_send, r1_buf, r2_buf, q32, acc_f, q_send, c1_buf, h_send,
    c2_buf, acc, fs, fr, gs, gr,
    load_sem, pool_sem, r1s, r1r, r2s, r2r, c1s, c1r, c2s, c2r, c3s, c3r, fws, fwr, f1s, f1r, f2s, f2r,
):
    row = lax.axis_index("row")
    col = lax.axis_index("col")
    ry, rz = row // 2, row % 2
    pos, core = col // 2, col % 2
    partner = pos * 2 + (1 - core)
    pool_rows = pool32.shape[0]

    def load(src, dst, n):
        return pltpu.make_async_copy(src, dst, load_sem.at[n])

    loads = {}
    loads["d3"] = load(d_hbm.at[3], d_raw.at[3], 0)
    loads["y3"] = load(b_hbm.at[3], y_buf.at[3], 1)
    loads["f5"] = load(f_hbm.at[5], f_raw.at[5], 2)
    loads["d2"] = load(d_hbm.at[2], d_raw.at[2], 3)
    loads["b"] = load(b_hbm.at[pl.ds(0, 3)], b_buf, 4)
    loads["cen"] = load(cen_hbm, cen, 5)
    for n in loads:
        loads[n].start()

    def pool_copy(n):
        return pltpu.make_async_copy(
            pool_hbm.at[pl.ds(n * 1024, 1024)], pool_in.at[n % 2], pool_sem.at[n % 2]
        )

    pool_copy(0).start()
    pool_copy(1).start()
    loads["d01"] = load(d_hbm.at[pl.ds(0, 2)], d_raw.at[pl.ds(0, 2)], 6)
    loads["f04"] = load(f_hbm.at[pl.ds(0, 5)], f_raw.at[pl.ds(0, 5)], 7)
    loads["d01"].start()
    loads["f04"].start()

    barrier = pltpu.get_barrier_semaphore()
    for d in range(1, 8):
        pl.semaphore_signal(barrier, inc=1, device_id=((row + d) % 8, col), device_id_type=MESH)
        pl.semaphore_signal(barrier, inc=1, device_id=(row, (col + 2 * d) % 16), device_id_type=MESH)
    pl.semaphore_signal(barrier, inc=1, device_id=(row, partner), device_id_type=MESH)
    pl.semaphore_wait(barrier, 15)

    def relayout_d(k):
        for t in range(2):
            for h in range(2):
                v = d_raw[k, t, h * 128 : (h + 1) * 128].reshape(512, 256).astype(F32)
                for u in range(2):
                    tmp32[u] = v[:, u * 128 : (u + 1) * 128]
                    for s in range(4):
                        lane = s * 256 + u * 128
                        d_mat[t * 256 + h * 128 : t * 256 + (h + 1) * 128, lane : lane + 128] = (
                            tmp32[u, pl.ds(s, 128, stride=4), :].astype(BF16)
                        )

    def relayout_f(slot):
        for t in range(4):
            v = f_raw[slot, t].reshape(512, 256).astype(F32)
            for u in range(2):
                tmp32[u] = v[:, u * 128 : (u + 1) * 128]
                for s in range(2):
                    lane = s * 256 + u * 128
                    f_mat[t * 256 : (t + 1) * 256, lane : lane + 128] = (
                        tmp32[u, pl.ds(s, 256, stride=2), :].astype(BF16)
                    )

    def pool_convert():
        for n in range(6):
            pool_copy(n).wait()

            @pl.loop(0, 16)
            def _(i):
                pool32[pl.ds(pl.multiple_of(n * 1024 + i * 64, 64), 64), :] = pool_in[
                    n % 2, pl.ds(pl.multiple_of(i * 64, 64), 64), :
                ].astype(F32)

            if n + 2 < 6:
                pool_copy(n + 2).start()

    def center_tile(p):
        which = jnp.int32(0)
        for l in range(1, 8):
            which = jnp.where(owner[l] == p, l, which)
        return which

    def center_squares():
        for p in range(8):
            v = cen[p].astype(F32)
            s = jnp.sum(v * v, axis=1, keepdims=True) * SLOPE
            csq[p] = jnp.transpose(jnp.broadcast_to(s, (256, 128)))[0:8, :]

    def score_item(n):
        base = pl.multiple_of(n * ROWS_ITEM, ROWS_ITEM)

        @pl.loop(0, ROWS_ITEM // 8)
        def _(i):
            for j in range(8):
                at = jnp.maximum(rows[base + i * 8 + j] - row * pool_rows, 0)
                stage32[pl.ds(i * 8 + j, 1), :] = pool32[pl.ds(at, 1), :]

        v = stage32[...]
        ssq = jnp.sum(v * v, axis=1, keepdims=True) * SLOPE
        vb = v.astype(BF16)

        @pl.loop(0, 4)
        def _(kk):
            for t in range(2):
                which = center_tile(kk * 2 + t)
                cross = lax.dot_general(
                    vb, cen[which], (((1,), (1,)), ((), ())), preferred_element_type=F32
                )
                e = (cross * (-2.0 * SLOPE) + ssq) + csq[which][0:1, :]
                k_mat[kk, pl.ds(base, ROWS_ITEM), t * 256 : (t + 1) * 256] = jnp.exp2(e).astype(BF16)

    loads["d3"].wait()
    loads["y3"].wait()
    relayout_d(3)
    for n in ("f5", "d2", "b", "cen", "d01", "f04"):
        loads[n].wait()
    pool_convert()
    center_squares()

    @pl.loop(0, 16)
    def _(n):
        score_item(n)

    @pl.loop(0, 4)
    def _(i):
        k = 3 - i
        part = jnp.dot(d_mat[...], y_buf[k].reshape(1024, 128), preferred_element_type=F32)
        p32[...] = part
        p_send[k] = part.astype(BF16)
        r1 = []
        for d in range(1, 4):
            to = (ry + d) % 4
            r1.append(pltpu.make_async_remote_copy(
                p_send.at[k, pl.ds(pl.multiple_of(to * 128, 128), 128)], r1_buf.at[k, ry],
                r1s.at[k, d], r1r.at[k, ry], device_id=(to * 2 + rz, col), device_id_type=MESH))
        for c in r1:
            c.start()

        @pl.when(k > 0)
        def _():
            relayout_f(jnp.maximum(k * (k - 1) // 2 + k - 1, 0))

        total = p32[pl.ds(pl.multiple_of(ry * 128, 128), 128), :]
        for d in range(1, 4):
            other = (ry + d) % 4
            pltpu.make_async_remote_copy(
                p_send.at[k, pl.ds(0, 128)], r1_buf.at[k, other],
                r1s.at[k, d], r1r.at[k, other], device_id=(row, col), device_id_type=MESH).wait_recv()
            total = total + r1_buf[k, other].astype(F32)
        r2_buf[k, row] = total.astype(BF16)
        r2 = []
        for d in range(1, 8):
            r2.append(pltpu.make_async_remote_copy(
                r2_buf.at[k, row], r2_buf.at[k, row],
                r2s.at[k, d], r2r.at[k, row], device_id=((row + d) % 8, col), device_id_type=MESH))
        for c in r2:
            c.start()
        for c in r1:
            c.wait_send()

        acc_f[...] = jnp.zeros_like(acc_f)

        for d in range(1, 8):
            other = (row + d) % 8
            pltpu.make_async_remote_copy(
                r2_buf.at[k, other], r2_buf.at[k, other],
                r2s.at[k, d], r2r.at[k, other], device_id=(row, col), device_id_type=MESH).wait_recv()
        for q in range(4):
            xq = r2_buf[k, 2 * q].astype(F32) + r2_buf[k, 2 * q + 1].astype(F32)
            alpha[k, q // 2, (q % 2) * 128 : (q % 2 + 1) * 128, :] = xq
            x_buf[k, q * 128 : (q + 1) * 128, :] = xq.astype(BF16)
        for c in r2:
            c.wait_send()

        @pl.when(k > 0)
        def _():
            prod = jnp.dot(f_mat[...], x_buf[k], preferred_element_type=F32)
            q32[...] = prod

            @pl.loop(k + 1, 4)
            def _(l):
                relayout_f(l * (l - 1) // 2 + k - 1)
                q32[...] += jnp.dot(f_mat[...], x_buf[l], preferred_element_type=F32)

            q_send[k] = q32[pl.ds(pl.multiple_of((1 - core) * 512, 512), 512), :].astype(BF16)
            c1 = pltpu.make_async_remote_copy(
                q_send.at[k], c1_buf.at[k], c1s.at[k], c1r.at[k],
                device_id=(row, partner), device_id_type=MESH)
            c1.start()
            c1.wait_recv()
            half = q32[pl.ds(pl.multiple_of(core * 512, 512), 512), :] + c1_buf[k].astype(F32)
            h_send[k] = half.astype(BF16)
            p32[...] = half
            c2 = []
            for d in range(1, 8):
                to = (pos + d) % 8
                c2.append(pltpu.make_async_remote_copy(
                    h_send.at[k, pl.ds(pl.multiple_of(to * 64, 64), 64)], c2_buf.at[k, pos],
                    c2s.at[k, d], c2r.at[k, pos], device_id=(row, to * 2 + core), device_id_type=MESH))
            for c in c2:
                c.start()
            c1.wait_send()
            relayout_d(k - 1)
            s = p32[pl.ds(pl.multiple_of(pos * 64, 64), 64), :]
            for d in range(1, 8):
                other = (pos + d) % 8
                pltpu.make_async_remote_copy(
                    h_send.at[k, pl.ds(0, 64)], c2_buf.at[k, other],
                    c2s.at[k, d], c2r.at[k, other], device_id=(row, col), device_id_type=MESH).wait_recv()
                s = s + c2_buf[k, other].astype(F32)
            own = pl.multiple_of(core * 512 + pos * 64, 64)
            mine_t, mine_a = own // 256, pl.multiple_of(own % 256, 64)
            target = b_buf[k - 1, mine_t, pl.ds(mine_a, 64), :].astype(F32)
            y_buf[k - 1, mine_t, pl.ds(mine_a, 64), :] = (target - s).astype(BF16)

            def y_at(half_of, p):
                o = half_of * 512 + p * 64
                return y_buf.at[k - 1, o // 256, pl.ds(pl.multiple_of(o % 256, 64), 64)]

            c3 = []
            for d in range(1, 8):
                c3.append(pltpu.make_async_remote_copy(
                    y_at(core, pos), y_at(core, pos), c3s.at[k, d], c3r.at[k, pos],
                    device_id=(row, (pos + d) % 8 * 2 + core), device_id_type=MESH))
            fw = [pltpu.make_async_remote_copy(
                y_at(core, pos), y_at(core, pos), fws.at[k, 0], fwr.at[k, pos],
                device_id=(row, partner), device_id_type=MESH)]
            for c in c3:
                c.start()
            fw[0].start()
            for c in c2:
                c.wait_send()
            for d in range(1, 8):
                other = (pos + d) % 8
                pltpu.make_async_remote_copy(
                    y_at(core, other), y_at(core, other), c3s.at[k, d], c3r.at[k, other],
                    device_id=(row, col), device_id_type=MESH).wait_recv()
                c = pltpu.make_async_remote_copy(
                    y_at(core, other), y_at(core, other), fws.at[k, d], fwr.at[k, other],
                    device_id=(row, partner), device_id_type=MESH)
                c.start()
                fw.append(c)
            for d in range(8):
                other = (pos + d) % 8
                pltpu.make_async_remote_copy(
                    y_at(1 - core, other), y_at(1 - core, other), fws.at[k, d], fwr.at[k, other],
                    device_id=(row, col), device_id_type=MESH).wait_recv()
            for c in c3 + fw:
                c.wait_send()

    @pl.loop(0, 16)
    def _(n):
        at = pl.ds(pl.multiple_of(n * 256, 256), 256)
        v = jnp.dot(k_mat[3, at, :], x_buf[3], preferred_element_type=F32)
        for kk in (2, 1):
            v = v + jnp.dot(k_mat[kk, at, :], x_buf[kk], preferred_element_type=F32)
        acc[at, :] = v

    def last(chunk):
        at = pl.ds(pl.multiple_of(chunk * 256, 256), 256)
        return acc[at, :] + jnp.dot(k_mat[0, at, :], x_buf[0], preferred_element_type=F32)

    def to_partner(p):
        return pltpu.make_async_remote_copy(
            fs.at[p], fr.at[p], f1s.at[p], f1r.at[p], device_id=(row, partner), device_id_type=MESH)

    def to_owner(p):
        return pltpu.make_async_remote_copy(
            gs.at[p], gr.at[pos], f2s.at[p], f2r.at[pos], device_id=(row, p * 2 + core), device_id_type=MESH)

    @pl.loop(1, 9)
    def _(d):
        p = (pos + d) % 8
        fs[p] = last(p * 2 + 1 - core).astype(BF16)
        to_partner(p).start()

    @pl.loop(1, 8)
    def _(d):
        p = (pos + d) % 8
        v = last(p * 2 + core)
        to_partner(p).wait_recv()
        gs[p] = (v + fr[p].astype(F32)).astype(BF16)
        to_owner(p).start()

    v = last(pos * 2 + core)
    to_partner(pos).wait_recv()
    v = v + fr[pos].astype(F32)
    for d in range(1, 8):
        other = (pos + d) % 8
        pltpu.make_async_remote_copy(
            gs.at[other], gr.at[other], f2s.at[other], f2r.at[other],
            device_id=(row, col), device_id_type=MESH).wait_recv()
        v = v + gr[other].astype(F32)
    pred[...] = v

    @pl.loop(1, 8)
    def _(d):
        p = (pos + d) % 8
        to_partner(p).wait_send()
        to_owner(p).wait_send()

    to_partner(pos).wait_send()


def shards(factor_blocks, inverse_blocks, right_side, centers, owner_map, test_pool, test_rows):
    any_ = pl.BlockSpec(memory_space=pl.ANY)
    smem = pl.BlockSpec(memory_space=pltpu.SMEM)
    vmem = pl.BlockSpec(memory_space=pltpu.VMEM)
    V = pltpu.VMEM
    dma = pltpu.SemaphoreType.DMA
    scratch = [
        V((6, 4, 256, 2, 256), BF16), V((4, 2, 256, 4, 256), BF16), V((1024, 512), BF16), V((512, 1024), BF16),
        V((2, 512, 128), F32), V((4, 4, 256, 128), BF16), V((3, 4, 256, 128), BF16), V((8, 256, 512), BF16),
        V((8, 8, 256), F32), V((2, 1024, 512), BF16), V((6144, 512), F32), V((ROWS_ITEM, 512), F32),
        V((4, 4096, 512), BF16), V((4, 512, 128), BF16), V((512, 128), F32), V((4, 512, 128), BF16),
        V((4, 4, 128, 128), BF16), V((4, 8, 128, 128), BF16), V((1024, 128), F32), V((8, 128), F32),
        V((4, 512, 128), BF16), V((4, 512, 128), BF16), V((4, 512, 128), BF16), V((4, 8, 64, 128), BF16),
        V((4096, 128), F32), V((8, 256, 128), BF16), V((8, 256, 128), BF16), V((8, 256, 128), BF16),
        V((8, 256, 128), BF16),
        dma((8,)), dma((2,)), dma((4, 4)), dma((4, 4)), dma((4, 8)), dma((4, 8)), dma((4,)), dma((4,)),
        dma((4, 8)), dma((4, 8)), dma((4, 8)), dma((4, 8)), dma((4, 8)), dma((4, 8)),
        dma((8,)), dma((8,)), dma((8,)), dma((8,)),
    ]
    return pl.pallas_call(
        kernel,
        out_shape=(
            jax.ShapeDtypeStruct((4, 2, 256, 128), F32),
            jax.ShapeDtypeStruct((256, 128), F32),
        ),
        in_specs=[smem, smem, any_, any_, any_, any_, any_],
        out_specs=(vmem, vmem),
        scratch_shapes=scratch,
        name="solve_and_score",
        compiler_params=pltpu.CompilerParams(
            collective_id=0, has_side_effects=True, vmem_limit_bytes=67043328
        ),
    )(owner_map.reshape(8), test_rows, factor_blocks, inverse_blocks, right_side, centers, test_pool)


def solution(mesh):
    in_specs = (
        P(None, None, "row", None, "col"),
        P(None, None, "col", None, "row"),
        P(None, None, "row", None),
        P(None, "col", None),
        P(None, "col"),
        P("row", None),
        P("row"),
    )
    out_specs = (P(None, None, "col", None), P(("row", "col"), None))
    return jax.shard_map(shards, mesh=mesh, in_specs=in_specs, out_specs=out_specs, check_vma=False)
```

time: 819 us -> 163 us (0.20)
  waiting for transfers between devices: 702 us -> 0 us
  Pallas kernels: 0 us -> 158 us
  local copies, waits for them, and re-layouts: 50.3 us -> 3.84 us
  matrix products: 36.4 us -> 0 us
  between operations: 14.3 us -> 0.64 us
  other arithmetic: 12.6 us -> 0 us
    psum x7 -> x0, waiting for transfers between devices: 640 us -> none  [the longest x3 334 us: subtract(): summed = lax.psum(partial_value, 'col')]
    pallas_call x0 -> x1, Pallas kernels: none -> 158 us  [shards(): pl.pallas_call(kernel, out_shape=(jax.ShapeDtypeStruct((4, 2, 256, 128),...]
    reduce_scatter x1 -> x0, waiting for transfers between devices: 61.2 us -> none  [shards(): lax.psum_scatter(jnp.dot(kernel, paired, preferred_element_type=jnp.float...]
    dot_general x11 -> x0, matrix products: 36.4 us -> none  [the longest x1 17.1 us: shards(): jnp.dot(kernel, paired, preferred_element_type=jnp.float32)]
    gather x2 -> x0, local copies, waits for them, and re-layouts: 22.5 us -> none  [the longest x1 21 us: shards(): span_rows = jnp.take(test_pool, located, axis=0)]
    slice x3 -> x0, local copies, waits for them, and re-layouts: 12.1 us -> none  [the longest x1 7.21 us: shards(): blocks[pair_slot(current, successor)]]
    unnamed x39 -> x2, local copies, waits for them, and re-layouts: 15 us -> 3.84 us
  transfers between devices with their start and end apart: 8 -> 0, of which waited for: 8 -> 0; matrix products, arithmetic and copies ran while one was open for 6% -> 0% of each run, Pallas kernels for 0% -> 0%
where the time goes in v1:
time: 163 us
  Pallas kernels  158 us (97%)
  local copies, waits for them, and re-layouts  3.84 us (2%)
    pallas_call x1, Pallas kernels, shards(): pl.pallas_call(kernel, out_shape=(jax.ShapeDtypeStruct((4, 2, 256, 128),...  158 us
    unnamed x2, local copies, waits for them, and re-layouts  3.84 us

profile of v1, /device:TPU:1, one launch (start us, length us, event | category | flops | bytes accessed | tf_op | source)
XLA Modules:
  0.0 162.9 jit_solution(17257314664069389422)
XLA Ops:
  0.6 158.4 %solve_and_score.1 = (f32[4,2,256,128]{3,2,1,0:T(8,128)}, f32[256,128]{1,0:T(8,128)}) custom-call(s32[8]{0:T(128)} %bitcast.1, s32[4096]{0:T(1024)} %rows.1, bf16[6,4,256,2,256]{4,3,2,1,0:T(2,128)(2,1)} %f_hbm.1, bf16[4,2,256,4,256]{4,3,2,1,0:T(4,128)(2,1)} %d_hbm.1, bf16[4,4,256,128]{3,2,1,0:T(8,128)(2,1)} %b_hbm.1, bf16[8,256,512]{2,1,0:T(8,128)(2,1)} %cen_hbm.1, ...), custom_call_target="tpu_custom_call" | custom-call | tf_op jit(solution)/shard_map/solve_and_score/pallas_call | solution.py:347
  159.1 2.3 %copy.11 = f32[4,2,256,128]{3,2,1,0:T(8,128)} copy(f32[4,2,256,128]{3,2,1,0:T(8,128)} %get-tuple-element.4) | data formatting | bytes 2097152
  161.3 1.6 copy.12

commit v2 on v1

--- a/solution.py
+++ b/solution.py
@@ -11,14 +11,37 @@
 F32 = jnp.float32
 BF16 = jnp.bfloat16
 SLOPE = -0.35 * 1.4426950408889634
-ROWS_ITEM = 256
+ROWS_ITEM = 512
+GATHERS = ((0, 0, 1, 1), (0, 1, 1, 1), (0, 1, 0, 1), (1, 0, 0, 0))
+PIECES = ((0, 0, 2, 4), (2, 4, 2, 4), (2, 2, 2, 4), (1, 3, 0, 0))
+
+
+def starts(plan):
+    out, done = [], 0
+    for counts in plan:
+        out.append([])
+        for count in counts:
+            out[-1].append(done)
+            done += count
+    return out, done
+
+
+def at_step(i, values):
+    d = list(values)
+    steps = []
+    while d:
+        steps.append(d[0])
+        d = [d[n + 1] - d[n] for n in range(len(d) - 1)]
+    pair = lax.div(i * (i - 1), 2)
+    triple = lax.div(i * (i - 1) * (i - 2), 6)
+    return steps[0] + steps[1] * i + steps[2] * pair + steps[3] * triple
 
 
 def kernel(
     owner, rows, f_hbm, d_hbm, b_hbm, cen_hbm, pool_hbm,
     alpha, pred,
-    f_raw, d_raw, f_mat, d_mat, tmp32, y_buf, b_buf, cen, csq, pool_in, pool32,
-    stage32, k_mat, x_buf, p32, p_send, r1_buf, r2_buf, q32, acc_f, q_send, c1_buf, h_send,
+    f_raw, d_raw, f_mat, d_mat, tmp32, y_buf, b_buf, cen, csq, pool_in, pool4,
+    stage4, span, ssq, k_mat, x_buf, p32, p_send, r1_buf, r2_buf, q32, acc_f, q_send, c1_buf, h_send,
     c2_buf, acc, fs, fr, gs, gr,
     load_sem, pool_sem, r1s, r1r, r2s, r2r, c1s, c1r, c2s, c2r, c3s, c3r, fws, fwr, f1s, f1r, f2s, f2r,
 ):
@@ -27,7 +50,7 @@
     ry, rz = row // 2, row % 2
     pos, core = col // 2, col % 2
     partner = pos * 2 + (1 - core)
-    pool_rows = pool32.shape[0]
+    pool_rows = pool4.shape[0] // 4
 
     def load(src, dst, n):
         return pltpu.make_async_copy(src, dst, load_sem.at[n])
@@ -59,7 +82,6 @@
         pl.semaphore_signal(barrier, inc=1, device_id=((row + d) % 8, col), device_id_type=MESH)
         pl.semaphore_signal(barrier, inc=1, device_id=(row, (col + 2 * d) % 16), device_id_type=MESH)
     pl.semaphore_signal(barrier, inc=1, device_id=(row, partner), device_id_type=MESH)
-    pl.semaphore_wait(barrier, 15)
 
     def relayout_d(k):
         for t in range(2):
@@ -90,9 +112,10 @@
 
             @pl.loop(0, 16)
             def _(i):
-                pool32[pl.ds(pl.multiple_of(n * 1024 + i * 64, 64), 64), :] = pool_in[
-                    n % 2, pl.ds(pl.multiple_of(i * 64, 64), 64), :
-                ].astype(F32)
+                v = pool_in[n % 2, pl.ds(pl.multiple_of(i * 64, 64), 64), :].astype(F32)
+                for q in range(4):
+                    at = pl.multiple_of(n * 4096 + i * 256, 256)
+                    pool4[pl.ds(at + q, 64, stride=4), :] = v[:, q * 128 : (q + 1) * 128]
 
             if n + 2 < 6:
                 pool_copy(n + 2).start()
@@ -109,47 +132,73 @@
             s = jnp.sum(v * v, axis=1, keepdims=True) * SLOPE
             csq[p] = jnp.transpose(jnp.broadcast_to(s, (256, 128)))[0:8, :]
 
-    def score_item(n):
+    def gather_item(n):
         base = pl.multiple_of(n * ROWS_ITEM, ROWS_ITEM)
 
-        @pl.loop(0, ROWS_ITEM // 8)
+        @pl.loop(0, ROWS_ITEM // 16)
         def _(i):
-            for j in range(8):
-                at = jnp.maximum(rows[base + i * 8 + j] - row * pool_rows, 0)
-                stage32[pl.ds(i * 8 + j, 1), :] = pool32[pl.ds(at, 1), :]
-
-        v = stage32[...]
-        ssq = jnp.sum(v * v, axis=1, keepdims=True) * SLOPE
-        vb = v.astype(BF16)
-
-        @pl.loop(0, 4)
-        def _(kk):
-            for t in range(2):
-                which = center_tile(kk * 2 + t)
-                cross = lax.dot_general(
-                    vb, cen[which], (((1,), (1,)), ((), ())), preferred_element_type=F32
+            for j in range(16):
+                at = jnp.maximum(rows[base + i * 16 + j] - row * pool_rows, 0)
+                stage4[pl.ds(pl.multiple_of((i * 16 + j) * 4, 4), 4), :] = pool4[
+                    pl.ds(at * 4, 4), :
+                ]
+
+        slot = lax.rem(n, 2)
+        total = None
+        for q in range(4):
+            v = stage4[pl.ds(q, ROWS_ITEM, stride=4), :]
+            span[slot, :, q * 128 : (q + 1) * 128] = v.astype(BF16)
+            total = v * v if total is None else total + v * v
+        total = jnp.sum(total, axis=1, keepdims=True) * SLOPE
+        ssq[slot] = jnp.broadcast_to(total, (ROWS_ITEM, 128))
+
+    def score_item(n, kk):
+        slot = lax.rem(n, 2)
+        base = pl.multiple_of(n * ROWS_ITEM, ROWS_ITEM)
+        for t in range(2):
+            which = center_tile(kk * 2 + t)
+            cross = lax.dot_general(
+                span[slot], cen[which], (((1,), (1,)), ((), ())), preferred_element_type=F32
+            )
+            for u in range(2):
+                lanes = slice(u * 128, (u + 1) * 128)
+                e = (cross[:, lanes] * (-2.0 * SLOPE) + ssq[slot]) + csq[which][0:1, lanes]
+                k_mat[kk, pl.ds(base, ROWS_ITEM), t * 256 + u * 128 : t * 256 + (u + 1) * 128] = (
+                    jnp.exp2(e).astype(BF16)
                 )
-                e = (cross * (-2.0 * SLOPE) + ssq) + csq[which][0:1, :]
-                k_mat[kk, pl.ds(base, ROWS_ITEM), t * 256 : (t + 1) * 256] = jnp.exp2(e).astype(BF16)
+
+    gather_at, gathers = starts(GATHERS)
+    piece_at, pieces = starts(PIECES)
+    assert gathers * ROWS_ITEM == k_mat.shape[1] and pieces == 4 * gathers
+
+    def score_work(i, site):
+        first = at_step(i, [at[site] for at in gather_at])
+
+        @pl.loop(first, first + at_step(i, [panel[site] for panel in GATHERS]))
+        def _(n):
+            gather_item(n)
+
+        first = at_step(i, [at[site] for at in piece_at])
+
+        @pl.loop(first, first + at_step(i, [panel[site] for panel in PIECES]))
+        def _(u):
+            n = lax.div(u, 4)
+            score_item(n, u - n * 4)
 
     loads["d3"].wait()
     loads["y3"].wait()
     relayout_d(3)
-    for n in ("f5", "d2", "b", "cen", "d01", "f04"):
-        loads[n].wait()
-    pool_convert()
-    center_squares()
-
-    @pl.loop(0, 16)
-    def _(n):
-        score_item(n)
-
     @pl.loop(0, 4)
     def _(i):
         k = 3 - i
         part = jnp.dot(d_mat[...], y_buf[k].reshape(1024, 128), preferred_element_type=F32)
         p32[...] = part
         p_send[k] = part.astype(BF16)
+
+        @pl.when(i == 0)
+        def _():
+            pl.semaphore_wait(barrier, 15)
+
         r1 = []
         for d in range(1, 4):
             to = (ry + d) % 4
@@ -159,9 +208,7 @@
         for c in r1:
             c.start()
 
-        @pl.when(k > 0)
-        def _():
-            relayout_f(jnp.maximum(k * (k - 1) // 2 + k - 1, 0))
+        score_work(i, 0)
 
         total = p32[pl.ds(pl.multiple_of(ry * 128, 128), 128), :]
         for d in range(1, 4):
@@ -181,7 +228,38 @@
         for c in r1:
             c.wait_send()
 
-        acc_f[...] = jnp.zeros_like(acc_f)
+        @pl.when(i == 0)
+        def _():
+            loads["f5"].wait()
+            loads["cen"].wait()
+            center_squares()
+
+        @pl.when(k > 0)
+        def _():
+            q32[...] = jnp.zeros_like(q32)
+
+            @pl.loop(k + 1, 4)
+            def _(l):
+                relayout_f(l * (l - 1) // 2 + k - 1)
+                q32[...] += jnp.dot(f_mat[...], x_buf[l], preferred_element_type=F32)
+
+            relayout_f(k * (k - 1) // 2 + k - 1)
+
+        @pl.when(i == 0)
+        def _():
+            pool_convert()
+
+        score_work(i, 1)
+
+        @pl.when(k == 0)
+        def _():
+            @pl.loop(0, 16)
+            def _(n):
+                at = pl.ds(pl.multiple_of(n * 256, 256), 256)
+                v = jnp.dot(k_mat[3, at, :], x_buf[3], preferred_element_type=F32)
+                for kk in (2, 1):
+                    v = v + jnp.dot(k_mat[kk, at, :], x_buf[kk], preferred_element_type=F32)
+                acc[at, :] = v
 
         for d in range(1, 8):
             other = (row + d) % 8
@@ -197,14 +275,7 @@
 
         @pl.when(k > 0)
         def _():
-            prod = jnp.dot(f_mat[...], x_buf[k], preferred_element_type=F32)
-            q32[...] = prod
-
-            @pl.loop(k + 1, 4)
-            def _(l):
-                relayout_f(l * (l - 1) // 2 + k - 1)
-                q32[...] += jnp.dot(f_mat[...], x_buf[l], preferred_element_type=F32)
-
+            q32[...] += jnp.dot(f_mat[...], x_buf[k], preferred_element_type=F32)
             q_send[k] = q32[pl.ds(pl.multiple_of((1 - core) * 512, 512), 512), :].astype(BF16)
             c1 = pltpu.make_async_remote_copy(
                 q_send.at[k], c1_buf.at[k], c1s.at[k], c1r.at[k],
@@ -223,7 +294,14 @@
             for c in c2:
                 c.start()
             c1.wait_send()
+
+            @pl.when(i == 0)
+            def _():
+                loads["d2"].wait()
+                loads["b"].wait()
+
             relayout_d(k - 1)
+            score_work(i, 2)
             s = p32[pl.ds(pl.multiple_of(pos * 64, 64), 64), :]
             for d in range(1, 8):
                 other = (pos + d) % 8
@@ -253,6 +331,13 @@
             fw[0].start()
             for c in c2:
                 c.wait_send()
+
+            @pl.when(i == 0)
+            def _():
+                loads["d01"].wait()
+                loads["f04"].wait()
+
+            score_work(i, 3)
             for d in range(1, 8):
                 other = (pos + d) % 8
                 pltpu.make_async_remote_copy(
@@ -271,14 +356,6 @@
             for c in c3 + fw:
                 c.wait_send()
 
-    @pl.loop(0, 16)
-    def _(n):
-        at = pl.ds(pl.multiple_of(n * 256, 256), 256)
-        v = jnp.dot(k_mat[3, at, :], x_buf[3], preferred_element_type=F32)
-        for kk in (2, 1):
-            v = v + jnp.dot(k_mat[kk, at, :], x_buf[kk], preferred_element_type=F32)
-        acc[at, :] = v
-
     def last(chunk):
         at = pl.ds(pl.multiple_of(chunk * 256, 256), 256)
         return acc[at, :] + jnp.dot(k_mat[0, at, :], x_buf[0], preferred_element_type=F32)
@@ -334,7 +411,8 @@
     scratch = [
         V((6, 4, 256, 2, 256), BF16), V((4, 2, 256, 4, 256), BF16), V((1024, 512), BF16), V((512, 1024), BF16),
         V((2, 512, 128), F32), V((4, 4, 256, 128), BF16), V((3, 4, 256, 128), BF16), V((8, 256, 512), BF16),
-        V((8, 8, 256), F32), V((2, 1024, 512), BF16), V((6144, 512), F32), V((ROWS_ITEM, 512), F32),
+        V((8, 8, 256), F32), V((2, 1024, 512), BF16), V((6144 * 4, 128), F32), V((ROWS_ITEM * 4, 128), F32),
+        V((2, ROWS_ITEM, 512), BF16), V((2, ROWS_ITEM, 128), F32),
         V((4, 4096, 512), BF16), V((4, 512, 128), BF16), V((512, 128), F32), V((4, 512, 128), BF16),
         V((4, 4, 128, 128), BF16), V((4, 8, 128, 128), BF16), V((1024, 128), F32), V((8, 128), F32),
         V((4, 512, 128), BF16), V((4, 512, 128), BF16), V((4, 512, 128), BF16), V((4, 8, 64, 128), BF16),

time: 163 us -> 104 us (0.64)
  Pallas kernels: 158 us -> 99.2 us
    pallas_call x1, Pallas kernels: 158 us -> 99.2 us  [shards(): pl.pallas_call(kernel, out_shape=(jax.ShapeDtypeStruct((4, 2, 256, 128),...]
where the time goes in v2:
time: 104 us
  Pallas kernels  99.2 us (95%)
  local copies, waits for them, and re-layouts  3.84 us (4%)
    pallas_call x1, Pallas kernels, shards(): pl.pallas_call(kernel, out_shape=(jax.ShapeDtypeStruct((4, 2, 256, 128),...  99.2 us
    unnamed x2, local copies, waits for them, and re-layouts  3.84 us

profile of v2, /device:TPU:1, one launch (start us, length us, event | category | flops | bytes accessed | tf_op | source)
XLA Modules:
  0.0 103.7 jit_solution(2439682475754458967)
XLA Ops:
  0.6 99.2 %solve_and_score.1 = (f32[4,2,256,128]{3,2,1,0:T(8,128)}, f32[256,128]{1,0:T(8,128)}) custom-call(s32[8]{0:T(128)} %bitcast.1, s32[4096]{0:T(1024)} %rows.1, bf16[6,4,256,2,256]{4,3,2,1,0:T(2,128)(2,1)} %f_hbm.1, bf16[4,2,256,4,256]{4,3,2,1,0:T(4,128)(2,1)} %d_hbm.1, bf16[4,4,256,128]{3,2,1,0:T(8,128)(2,1)} %b_hbm.1, bf16[8,256,512]{2,1,0:T(8,128)(2,1)} %cen_hbm.1, ...), custom_call_target="tpu_custom_call" | custom-call | tf_op jit(solution)/shard_map/solve_and_score/pallas_call | solution.py:425
  99.9 2.3 %copy.11 = f32[4,2,256,128]{3,2,1,0:T(8,128)} copy(f32[4,2,256,128]{3,2,1,0:T(8,128)} %get-tuple-element.4) | data formatting | bytes 2097152
  102.2 1.6 %copy.12 = f32[256,128]{1,0:T(8,128)} copy(f32[256,128]{1,0:T(8,128)} %get-tuple-element.5) | data formatting | bytes 262144

commit v3 on v2

--- a/solution.py
+++ b/solution.py
@@ -14,6 +14,11 @@
 ROWS_ITEM = 512
 GATHERS = ((0, 0, 1, 1), (0, 1, 1, 1), (0, 1, 0, 1), (1, 0, 0, 0))
 PIECES = ((0, 0, 2, 4), (2, 4, 2, 4), (2, 2, 2, 4), (1, 3, 0, 0))
+
+
+FAR = ((2, 1), (1, 1), (3, 1), (2, 0), (1, 0), (3, 0), (0, 1))
+NEAR = FAR[::-1]
+ROW_FAR = ((2, 1), (1, 1), (3, 1), (0, 1), (2, 0), (1, 0), (3, 0))
 
 
 def starts(plan):
@@ -50,6 +55,13 @@
     ry, rz = row // 2, row % 2
     pos, core = col // 2, col % 2
     partner = pos * 2 + (1 - core)
+
+    def row_at(step):
+        return (ry + step[0]) % 4 * 2 + (rz + step[1]) % 2
+
+    def pos_at(step):
+        return (pos // 2 + step[0]) % 4 * 2 + (pos % 2 + step[1]) % 2
+
     pool_rows = pool4.shape[0] // 4
 
     def load(src, dst, n):
@@ -191,26 +203,39 @@
     @pl.loop(0, 4)
     def _(i):
         k = 3 - i
-        part = jnp.dot(d_mat[...], y_buf[k].reshape(1024, 128), preferred_element_type=F32)
-        p32[...] = part
-        p_send[k] = part.astype(BF16)
+        rhs = y_buf[k].reshape(1024, 128)
+
+        def quarter(d):
+            return pl.ds(pl.multiple_of((ry + d) % 4 * 128, 128), 128)
+
+        def pair(d, e):
+            lhs = jnp.concatenate([d_mat[quarter(d), :], d_mat[quarter(e), :]], axis=0)
+            return jnp.dot(lhs, rhs, preferred_element_type=F32)
+
+        def first_exchange(d):
+            return pltpu.make_async_remote_copy(
+                p_send.at[k, quarter(d)], r1_buf.at[k, ry],
+                r1s.at[k, d], r1r.at[k, ry], device_id=((ry + d) % 4 * 2 + rz, col), device_id_type=MESH)
+
+        part = pair(2, 1)
+        p_send[k, quarter(2), :] = part[0:128].astype(BF16)
+        p_send[k, quarter(1), :] = part[128:256].astype(BF16)
 
         @pl.when(i == 0)
         def _():
             pl.semaphore_wait(barrier, 15)
 
-        r1 = []
-        for d in range(1, 4):
-            to = (ry + d) % 4
-            r1.append(pltpu.make_async_remote_copy(
-                p_send.at[k, pl.ds(pl.multiple_of(to * 128, 128), 128)], r1_buf.at[k, ry],
-                r1s.at[k, d], r1r.at[k, ry], device_id=(to * 2 + rz, col), device_id_type=MESH))
-        for c in r1:
-            c.start()
+        r1 = [first_exchange(d) for d in (2, 1, 3)]
+        r1[0].start()
+        r1[1].start()
+        part = pair(3, 0)
+        p_send[k, quarter(3), :] = part[0:128].astype(BF16)
+        r1[2].start()
+        p32[0:128] = part[128:256]
 
         score_work(i, 0)
 
-        total = p32[pl.ds(pl.multiple_of(ry * 128, 128), 128), :]
+        total = p32[0:128]
         for d in range(1, 4):
             other = (ry + d) % 4
             pltpu.make_async_remote_copy(
@@ -219,10 +244,10 @@
             total = total + r1_buf[k, other].astype(F32)
         r2_buf[k, row] = total.astype(BF16)
         r2 = []
-        for d in range(1, 8):
+        for d, step in enumerate(ROW_FAR):
             r2.append(pltpu.make_async_remote_copy(
                 r2_buf.at[k, row], r2_buf.at[k, row],
-                r2s.at[k, d], r2r.at[k, row], device_id=((row + d) % 8, col), device_id_type=MESH))
+                r2s.at[k, d], r2r.at[k, row], device_id=(row_at(step), col), device_id_type=MESH))
         for c in r2:
             c.start()
         for c in r1:
@@ -275,19 +300,23 @@
 
         @pl.when(k > 0)
         def _():
-            q32[...] += jnp.dot(f_mat[...], x_buf[k], preferred_element_type=F32)
-            q_send[k] = q32[pl.ds(pl.multiple_of((1 - core) * 512, 512), 512), :].astype(BF16)
+            def half_product(which):
+                at = pl.ds(pl.multiple_of(which * 512, 512), 512)
+                return q32[at, :] + jnp.dot(f_mat[at, :], x_buf[k], preferred_element_type=F32)
+
+            q_send[k] = half_product(1 - core).astype(BF16)
             c1 = pltpu.make_async_remote_copy(
                 q_send.at[k], c1_buf.at[k], c1s.at[k], c1r.at[k],
                 device_id=(row, partner), device_id_type=MESH)
             c1.start()
+            p32[...] = half_product(core)
             c1.wait_recv()
-            half = q32[pl.ds(pl.multiple_of(core * 512, 512), 512), :] + c1_buf[k].astype(F32)
+            half = p32[...] + c1_buf[k].astype(F32)
             h_send[k] = half.astype(BF16)
             p32[...] = half
             c2 = []
-            for d in range(1, 8):
-                to = (pos + d) % 8
+            for d, step in enumerate(FAR):
+                to = pos_at(step)
                 c2.append(pltpu.make_async_remote_copy(
                     h_send.at[k, pl.ds(pl.multiple_of(to * 64, 64), 64)], c2_buf.at[k, pos],
                     c2s.at[k, d], c2r.at[k, pos], device_id=(row, to * 2 + core), device_id_type=MESH))
@@ -319,10 +348,10 @@
                 return y_buf.at[k - 1, o // 256, pl.ds(pl.multiple_of(o % 256, 64), 64)]
 
             c3 = []
-            for d in range(1, 8):
+            for d, step in enumerate(FAR):
                 c3.append(pltpu.make_async_remote_copy(
                     y_at(core, pos), y_at(core, pos), c3s.at[k, d], c3r.at[k, pos],
-                    device_id=(row, (pos + d) % 8 * 2 + core), device_id_type=MESH))
+                    device_id=(row, pos_at(step) * 2 + core), device_id_type=MESH))
             fw = [pltpu.make_async_remote_copy(
                 y_at(core, pos), y_at(core, pos), fws.at[k, 0], fwr.at[k, pos],
                 device_id=(row, partner), device_id_type=MESH)]
@@ -338,8 +367,8 @@
                 loads["f04"].wait()
 
             score_work(i, 3)
-            for d in range(1, 8):
-                other = (pos + d) % 8
+            for d, step in enumerate(NEAR, 1):
+                other = pos_at(step)
                 pltpu.make_async_remote_copy(
                     y_at(core, other), y_at(core, other), c3s.at[k, d], c3r.at[k, other],
                     device_id=(row, col), device_id_type=MESH).wait_recv()
@@ -368,16 +397,19 @@
         return pltpu.make_async_remote_copy(
             gs.at[p], gr.at[pos], f2s.at[p], f2r.at[pos], device_id=(row, p * 2 + core), device_id_type=MESH)
 
-    @pl.loop(1, 9)
-    def _(d):
-        p = (pos + d) % 8
+    def give(step):
+        p = pos_at(step)
         fs[p] = last(p * 2 + 1 - core).astype(BF16)
         to_partner(p).start()
 
-    @pl.loop(1, 8)
-    def _(d):
-        p = (pos + d) % 8
+    order = FAR + ((0, 0),)
+    give(order[0])
+    give(order[1])
+    for n, step in enumerate(FAR):
+        p = pos_at(step)
         v = last(p * 2 + core)
+        if n + 2 < len(order):
+            give(order[n + 2])
         to_partner(p).wait_recv()
         gs[p] = (v + fr[p].astype(F32)).astype(BF16)
         to_owner(p).start()
@@ -400,6 +432,11 @@
         to_owner(p).wait_send()
 
     to_partner(pos).wait_send()
+
+
+def finish(solved, scored, alpha, pred):
+    alpha[...] = solved[...]
+    pred[...] = scored[...]
 
 
 def shards(factor_blocks, inverse_blocks, right_side, centers, owner_map, test_pool, test_rows):
@@ -422,7 +459,7 @@
         dma((4, 8)), dma((4, 8)), dma((4, 8)), dma((4, 8)), dma((4, 8)), dma((4, 8)),
         dma((8,)), dma((8,)), dma((8,)), dma((8,)),
     ]
-    return pl.pallas_call(
+    solved, scored = pl.pallas_call(
         kernel,
         out_shape=(
             jax.ShapeDtypeStruct((4, 2, 256, 128), F32),
@@ -436,6 +473,16 @@
             collective_id=0, has_side_effects=True, vmem_limit_bytes=67043328
         ),
     )(owner_map.reshape(8), test_rows, factor_blocks, inverse_blocks, right_side, centers, test_pool)
+    return pl.pallas_call(
+        finish,
+        out_shape=(
+            jax.ShapeDtypeStruct((4, 2, 256, 128), F32),
+            jax.ShapeDtypeStruct((256, 128), F32),
+        ),
+        in_specs=[vmem, vmem],
+        out_specs=(vmem, vmem),
+        name="finish",
+    )(solved, scored)
 
 
 def solution(mesh):

time: 104 us -> 99.4 us (0.956)
  local copies, waits for them, and re-layouts: 3.84 us -> 0 us
    unnamed x2 -> x0, local copies, waits for them, and re-layouts: 3.84 us -> none
    pallas_call x1, Pallas kernels: 99.2 us -> 96.2 us  [shards(): pl.pallas_call(kernel, out_shape=(jax.ShapeDtypeStruct((4, 2, 256, 128),...]
    pallas_call x0 -> x1, Pallas kernels: none -> 2.3 us  [shards(): pl.pallas_call(finish, out_shape=(jax.ShapeDtypeStruct((4, 2, 256, 128),...]
where the time goes in v3:
time: 99.4 us; the launch traced here: 99.1 us
  Pallas kernels  98.5 us (99%)
    pallas_call x1, Pallas kernels, shards(): pl.pallas_call(kernel, out_shape=(jax.ShapeDtypeStruct((4, 2, 256, 128),...  96.2 us
    pallas_call x1, Pallas kernels, shards(): pl.pallas_call(finish, out_shape=(jax.ShapeDtypeStruct((4, 2, 256, 128),...  2.3 us

profile of v3, /device:TPU:1, one launch (start us, length us, event | category | flops | bytes accessed | tf_op | source)
XLA Modules:
  0.0 99.1 jit_solution(2551974623298444916)
XLA Ops:
  0.6 96.2 %solve_and_score.1 = (f32[4,2,256,128]{3,2,1,0:T(8,128)}, f32[256,128]{1,0:T(8,128)}) custom-call(s32[8]{0:T(128)} %bitcast.1, s32[4096]{0:T(1024)} %rows.1, bf16[6,4,256,2,256]{4,3,2,1,0:T(2,128)(2,1)} %f_hbm.1, bf16[4,2,256,4,256]{4,3,2,1,0:T(4,128)(2,1)} %d_hbm.1, bf16[4,4,256,128]{3,2,1,0:T(8,128)(2,1)} %b_hbm.1, bf16[8,256,512]{2,1,0:T(8,128)(2,1)} %cen_hbm.1, ...), custom_call_target="tpu_custom_call" | custom-call | tf_op jit(solution)/shard_map/solve_and_score/pallas_call | solution.py:462
  96.8 2.3 %finish.1 = (f32[4,2,256,128]{3,2,1,0:T(8,128)}, f32[256,128]{1,0:T(8,128)}) custom-call(f32[4,2,256,128]{3,2,1,0:T(8,128)} %get-tuple-element.4.solved, f32[256,128]{1,0:T(8,128)} %get-tuple-element.5.scored), custom_call_target="tpu_custom_call" | custom-call | tf_op jit(solution)/shard_map/finish/pallas_call | solution.py:476
